TPU v7x, 32 devices: a whole 2x2x4 slice. The times are simulated.
32 devices in a mesh: obj: 4 (over z), plane: 4 (over y, core), tile: 2 (over x).
Axes of the slice: x: 2, y: 2, z: 4, core: 2. Of those that a mesh axis runs over, the one named last changes fastest.
Arguments:
- tokens: bfloat16 [8, 3, 32, 32, 1024], P('obj', None, 'plane', 'tile'), may hold values from -6 to 6
- gout: bfloat16 [8, 3, 128, 128, 128], P('obj', None, 'plane', 'tile'), may hold values from -6 to 6
- deconv_weight: bfloat16 [1024, 2048], replicated, may hold values from -0.1875 to 0.1875
- deconv_bias: float32 [128], replicated, may hold values from -4 to 4
- conv_kernels: bfloat16 [2, 1152, 128], replicated, may hold values from -0.1875 to 0.1875
- conv_biases: float32 [2, 128], replicated, may hold values from -4 to 4
Outputs:
- d_tokens: bfloat16 [8, 3, 32, 32, 1024], P('obj', None, 'plane', 'tile')
- d_deconv_weight: float32 [1024, 2048], P(('obj', 'plane', 'tile'))
- d_deconv_bias: float32 [128], replicated
- d_conv_kernels: float32 [2, 1152, 128], replicated
- d_conv_biases: float32 [2, 128], replicated
All inputs are finite; a program needn't handle non-finite values.
Results may differ from a plain program's by a relative error of at most 0.01.
Values may be sent and summed in bfloat16 or wider, within the bound.
No kernel may reach another device: no remote copies, remote signals or barrier semaphores. Data moves between devices by JAX's collectives and lax.ppermute only.
A program may use at most 192 MiB of HBM per device.

v0:
```python
import jax
import jax.numpy as jnp
from jax import lax
from jax.sharding import PartitionSpec as P


def padded_2(array, sides, width):
    for axis, dim in sides:
        size, length = (lax.axis_size(axis), array.shape[dim])
        up = [(i, (i + 1) % size) for i in range(size - 1)]
        down = [(j, i) for i, j in up]
        last = lax.slice_in_dim(array, length - width, length, axis=dim)
        initial = lax.slice_in_dim(array, 0, width, axis=dim)
        before = lax.ppermute(last, axis, up)
        after = lax.ppermute(initial, axis, down)
        array = jnp.concatenate([before, array, after], axis=dim)
    return array


def columns(padded, height, breadth, flipped):
    pieces = []
    for tap_y in range(3):
        for tap_x in range(3):
            shift_y = 2 - tap_y if flipped else tap_y
            shift_x = 2 - tap_x if flipped else tap_x
            pieces.append(padded[..., shift_y : shift_y + height, shift_x : shift_x + breadth, :])
    return jnp.concatenate(pieces, axis=-1)


def convolve(padded, kernel, height, breadth, flipped):
    gathered = columns(padded, height, breadth, flipped)
    products = jnp.dot(
        gathered.reshape(-1, gathered.shape[-1]), kernel, preferred_element_type=jnp.float32
    )
    return products.reshape(padded.shape[:-3] + (height, breadth, kernel.shape[1]))


def upsample(tokens_here, weight, offsets):
    planes, tok_rows, tok_cols, fan_width = tokens_here.shape
    products = jnp.dot(
        tokens_here.reshape(-1, fan_width), weight, preferred_element_type=jnp.float32
    )
    products = products.reshape(planes, tok_rows, tok_cols, 4, 4, -1).transpose(0, 1, 3, 2, 4, 5)
    return products.reshape(planes, 4 * tok_rows, 4 * tok_cols, -1) + offsets


def tap_layout(gradient):
    planes, height, breadth, channels = gradient.shape
    blocks = gradient.reshape(planes, height // 4, 4, breadth // 4, 4, channels).transpose(
        0, 1, 3, 2, 4, 5
    )
    return blocks.reshape(-1, 16 * channels)


def contexts(row_sum, col_sum, extent):
    row_mean = row_sum / extent
    col_mean = col_sum / extent
    row_ctx = jnp.stack([row_mean[1], row_mean[0], col_mean[0]])
    col_ctx = jnp.stack([row_mean[2], col_mean[2], col_mean[1]])
    return (row_ctx, col_ctx)


def adjoint_contexts(row_sum, col_sum, extent):
    row_adjoint = jnp.stack([row_sum[1], row_sum[0], col_sum[0]])
    col_adjoint = jnp.stack([row_sum[2], col_sum[2], col_sum[1]])
    return (row_adjoint / extent, col_adjoint / extent)


def flip_kernel(kernel):
    channels = kernel.shape[1]
    return kernel.reshape(9, channels, channels).transpose(0, 2, 1).reshape(9 * channels, channels)


def pooled_sums(row_part, col_part, row_start, col_start, extent):
    zero_index = jnp.zeros((), jnp.int32)
    row_full = lax.dynamic_update_slice(
        jnp.zeros((row_part.shape[0], extent, row_part.shape[2]), jnp.float32),
        row_part,
        (zero_index, row_start, zero_index),
    )
    col_full = lax.dynamic_update_slice(
        jnp.zeros((col_part.shape[0], extent, col_part.shape[2]), jnp.float32),
        col_part,
        (zero_index, col_start, zero_index),
    )
    result = lax.psum((row_full, col_full), ("plane", "tile"))
    return result


def object_pass(tokens_here, grad_out, deconv_weight, deconv_bias, conv_kernels, conv_biases):
    hidden = upsample(tokens_here, deconv_weight, deconv_bias)
    planes, height, breadth, channels = hidden.shape
    extent = height * lax.axis_size("plane")
    row_start = lax.axis_index("plane") * height
    col_start = lax.axis_index("tile") * breadth
    layers = conv_kernels.shape[0]
    stored = []
    for layer_index in range(layers):
        row_sum, col_sum = pooled_sums(
            jnp.sum(hidden, 2), jnp.sum(hidden, 1), row_start, col_start, extent
        )
        row_ctx, col_ctx = contexts(row_sum, col_sum, extent)
        row_band = lax.dynamic_slice_in_dim(row_ctx, row_start, height, 1)
        col_band = lax.dynamic_slice_in_dim(col_ctx, col_start, breadth, 1)
        preact = hidden + row_band[:, :, None, :] + col_band[:, None, :, :]
        activated = jax.nn.silu(preact).astype(jnp.bfloat16)
        padded = padded_2(activated, (("plane", 1), ("tile", 2)), 1)
        conv_out = convolve(padded, conv_kernels[layer_index], height, breadth, False)
        hidden = hidden + conv_out + conv_biases[layer_index]
        stored.append((preact, padded))
    gradient = grad_out.astype(jnp.float32)
    kernel_grads = []
    bias_grads = []
    for layer_index in reversed(range(layers)):
        preact, padded = stored[layer_index]
        grad_bf = gradient.astype(jnp.bfloat16)
        bias_grads.insert(0, jnp.sum(gradient, (0, 1, 2)))
        grad_pad = padded_2(grad_bf, (("plane", 1), ("tile", 2)), 1)
        act_grad = convolve(grad_pad, flip_kernel(conv_kernels[layer_index]), height, breadth, True)
        gathered = columns(padded, height, breadth, False)
        kernel_grads.insert(
            0,
            lax.dot_general(
                gathered.reshape(-1, gathered.shape[-1]),
                grad_bf.reshape(-1, channels),
                (((0,), (0,)), ((), ())),
                preferred_element_type=jnp.float32,
            ),
        )
        sigmoid_pre = jax.nn.sigmoid(preact)
        pre_grad = act_grad * sigmoid_pre * (1.0 + preact * (1.0 - sigmoid_pre))
        row_sum, col_sum = pooled_sums(
            jnp.sum(pre_grad, 2), jnp.sum(pre_grad, 1), row_start, col_start, extent
        )
        row_adjoint, col_adjoint = adjoint_contexts(row_sum, col_sum, extent)
        row_band = lax.dynamic_slice_in_dim(row_adjoint, row_start, height, 1)
        col_band = lax.dynamic_slice_in_dim(col_adjoint, col_start, breadth, 1)
        gradient = gradient + pre_grad + row_band[:, :, None, :] + col_band[:, None, :, :]
    grad_bf = gradient.astype(jnp.bfloat16)
    tap_grads = tap_layout(grad_bf)
    tok_grad = lax.dot_general(
        tap_grads, deconv_weight, (((1,), (1,)), ((), ())), preferred_element_type=jnp.float32
    )
    tok_grad = tok_grad.astype(jnp.bfloat16).reshape(tokens_here.shape)
    return (
        tok_grad,
        tap_grads,
        jnp.sum(gradient, (0, 1, 2)),
        jnp.stack(kernel_grads),
        jnp.stack(bias_grads),
    )


def per_device(tokens, gout, deconv_weight, deconv_bias, conv_kernels, conv_biases):
    tok_list = []
    tap_list = []
    flat_list = []
    bias_grad = jnp.zeros((deconv_bias.shape[0],), jnp.float32)
    kernel_sum = jnp.zeros(conv_kernels.shape, jnp.float32)
    conv_bias_sum = jnp.zeros(conv_biases.shape, jnp.float32)
    for object_index in range(tokens.shape[0]):
        tokens_here = tokens[object_index]
        tok_grad, tap_grads, bias_part, kernel_part, conv_bias_part = object_pass(
            tokens_here, gout[object_index], deconv_weight, deconv_bias, conv_kernels, conv_biases
        )
        tok_list.append(tok_grad)
        tap_list.append(tap_grads)
        flat_list.append(tokens_here.reshape(-1, tokens_here.shape[-1]))
        bias_grad = bias_grad + bias_part
        kernel_sum = kernel_sum + kernel_part
        conv_bias_sum = conv_bias_sum + conv_bias_part
    tok_out = jnp.stack(tok_list)
    tap_all = jnp.concatenate(tap_list, axis=0)
    tok_flat = jnp.concatenate(flat_list, axis=0)
    object_part = lax.psum_scatter(
        lax.dot_general(
            tok_flat, tap_all, (((0,), (0,)), ((), ())), preferred_element_type=jnp.float32
        ).astype(jnp.bfloat16),
        "obj",
        scatter_dimension=0,
        tiled=True,
    ).astype(jnp.float32)
    weight_grad = lax.psum_scatter(object_part, ("plane", "tile"), scatter_dimension=0, tiled=True)
    kernel_total, conv_bias_total, bias_total = lax.psum(
        (kernel_sum, conv_bias_sum, bias_grad), ("obj", "plane", "tile")
    )
    return (tok_out, weight_grad, bias_total, kernel_total, conv_bias_total)


def solution(mesh):
    placed = (
        P("obj", None, "plane", "tile", None),
        P("obj", None, "plane", "tile", None),
        P(),
        P(),
        P(),
        P(),
    )
    return jax.shard_map(
        per_device,
        mesh=mesh,
        in_specs=placed,
        out_specs=(
            P("obj", None, "plane", "tile", None),
            P(("obj", "plane", "tile"), None),
            P(),
            P(),
            P(),
        ),
        check_vma=False,
    )
```

profile of v0, /device:TPU:0, one launch (start us, length us, event | category | flops | bytes accessed | tf_op | source)
XLA Modules:
  0.0 781.6 jit_solution(1945525639712762014)
XLA Ops:
  7.2 5.1 fusion.89
  13.1 3.0 collective-permute-start
  18.0 5.2 collective-permute-start.12
  24.5 7.7 dot_general.56
  32.2 7.5 copy.45
  39.7 4.0 convolution_bitcast_fusion.4
  43.8 4.3 add_reduce_fusion.2
  55.1 2.9 fusion.92
  59.8 3.1 copy.40
  65.7 5.1 copy.35
  71.7 3.4 collective-permute-start.15
  77.2 4.5 collective-permute-start.3
  83.5 3.3 maximum_maximum_fusion.3
  94.4 3.3 maximum_maximum_fusion
  101.3 2.8 constant_dynamic-update-slice_fusion
  108.9 3.9 copy-done.53
  118.9 3.9 multiply_convert_fusion.3
  122.8 2.9 collective-permute-start.16
  127.0 5.1 collective-permute-start.4
  135.1 4.6 collective-permute-start.18
  141.0 4.5 collective-permute-start.6
  153.3 2.3 pad_maximum_fusion.1
  170.7 5.7 fusion.88
  176.4 10.6 %fusion.85 = (f32[3,64,128]{2,1,0:T(8,128)S(1)}, f32[3,32,128]{2,1,0:T(8,128)S(1)}, f32[3,32,64,128]{3,2,1,0:T(8,128)}) fusion(f32[128]{0:T(128)S(1)} %slice_bitcast_fusion, bf16[3,32,64,1152]{3,2,1,0:T(8,128)(2,1)} %slice_dynamic-update-slice_fusion.36, bf16[2,1152,128]{2,1,0:T(8,128)(2,1)S(1)} %copy-done.25, f32[3,32,64,128]{3,2,1,0:T(8,128)S(1)} %bitcast.149, ...), kind=kOutput, calls=%fused_computation.314 | convolution fusion | flops 1815834624 | bytes 20890624 | tf_op jit(solution)/shard_map/dot_general | solution.py:32
  190.9 2.8 slice_dynamic-update-slice_fusion.24
  193.7 53.1 %all-reduce.17.cloned.1.call-done = (f32[3,128,128]{2,1,0:T(8,128)}, f32[3,128,128]{2,1,0:T(8,128)}, f32[3,128,128]{2,1,0:T(8,128)}, f32[3,128,128]{2,1,0:T(8,128)}) async-done(((f32[3,128,128]{2,1,0:T(8,128)}, f32[3,128,128]{2,1,0:T(8,128)}, f32[3,128,128]{2,1,0:T(8,128)}, f32[3,128,128]{2,1,0:T(8,128)}), (f32[3,128,128]{2,1,0:T(8,128)}, f32[3,128,128]{2,1,0:T(8,128)}, f32[3,128,128]{2,1,0:T(8,128)}, ...) | async-done | bytes 786448 | tf_op jit(solution)/shard_map/psum | solution.py:86
  250.9 2.7 multiply_convert_fusion
  253.7 12.2 %fusion.87 = (f32[3,64,128]{2,1,0:T(8,128)S(1)}, f32[3,32,128]{2,1,0:T(8,128)S(1)}, f32[3,32,64,128]{3,2,1,0:T(8,128)}) fusion(f32[3,64,128]{2,1,0:T(8,128)S(1)} %fusion.41, f32[3,32,64,128]{3,2,1,0:T(8,128)S(1)} %copy-done.13, f32[3,32,128]{2,1,0:T(8,128)S(1)} %fusion.61, bf16[3,32,64,1152]{3,2,1,0:T(8,128)(2,1)} %slice_dynamic-update-slice_fusion.24, ...), kind=kOutput, calls=%fused_computation.316 | convolution fusion | flops 1821339648 | bytes 21037056 | tf_op jit(solution)/shard_map/dot_general | solution.py:32
  266.8 6.6 fusion.84
  277.9 4.1 collective-permute-start.28
  289.6 4.5 collective-permute-start.26
  297.1 5.7 collective-permute-start.30
  302.9 3.0 pad_maximum_fusion.6
  313.3 32.7 %all-reduce.15.cloned.1.call-done = (f32[3,128,128]{2,1,0:T(8,128)}, f32[3,128,128]{2,1,0:T(8,128)}, f32[3,128,128]{2,1,0:T(8,128)}, f32[3,128,128]{2,1,0:T(8,128)}) async-done(((f32[3,128,128]{2,1,0:T(8,128)}, f32[3,128,128]{2,1,0:T(8,128)}, f32[3,128,128]{2,1,0:T(8,128)}, f32[3,128,128]{2,1,0:T(8,128)}), (f32[3,128,128]{2,1,0:T(8,128)}, f32[3,128,128]{2,1,0:T(8,128)}, f32[3,128,128]{2,1,0:T(8,128)}, ...) | async-done | bytes 786448 | tf_op jit(solution)/shard_map/psum | solution.py:86
  349.8 5.2 fusion.82
  357.6 4.1 collective-permute-start.8
  363.1 2.3 collective-permute-start.23
  366.9 4.5 collective-permute-start.11
  372.8 2.4 maximum_maximum_fusion.5
  380.3 2.6 maximum_maximum_fusion.2
  397.2 6.5 fusion.86
  403.7 11.7 %fusion.83 = (f32[3,64,128]{2,1,0:T(8,128)S(1)}, f32[3,32,128]{2,1,0:T(8,128)S(1)}, f32[3,32,64,128]{3,2,1,0:T(8,128)}) fusion(f32[3,64,128]{2,1,0:T(8,128)S(1)} %copy-done.46, f32[3,32,128]{2,1,0:T(8,128)S(1)} %copy-done.52, f32[3,32,64,128]{3,2,1,0:T(8,128)S(1)} %bitcast.150, f32[128]{0:T(128)S(1)} %copy-done.55, ...), kind=kOutput, calls=%fused_computation.312 | convolution fusion | flops 1822126080 | bytes 21037568 | tf_op jit(solution)/shard_map/dot_general | solution.py:32
  421.2 3.9 constant_dynamic-update-slice_fusion.6
  425.1 56.2 %all-reduce.13.cloned.1.call-done = (f32[3,128,128]{2,1,0:T(8,128)}, f32[3,128,128]{2,1,0:T(8,128)}, f32[3,128,128]{2,1,0:T(8,128)}, f32[3,128,128]{2,1,0:T(8,128)}) async-done(((f32[3,128,128]{2,1,0:T(8,128)}, f32[3,128,128]{2,1,0:T(8,128)}, f32[3,128,128]{2,1,0:T(8,128)}, f32[3,128,128]{2,1,0:T(8,128)}), (f32[3,128,128]{2,1,0:T(8,128)}, f32[3,128,128]{2,1,0:T(8,128)}, f32[3,128,128]{2,1,0:T(8,128)}, ...) | async-done | bytes 786448 | tf_op jit(solution)/shard_map/psum | solution.py:86
  485.1 7.8 fusion.79
  494.8 3.8 reshape.166
  498.6 3.2 copy.58
  501.8 3.9 reshape.169
  505.7 7.8 convolution_convert_fusion
  513.6 3.6 slice_dynamic-update-slice_fusion.8
  517.1 3.0 slice_dynamic-update-slice_fusion.7
  522.2 3.2 pad_maximum_fusion.7
  536.0 5.1 copy-done.54
  541.0 7.3 convolution_bitcast_fusion.3
  548.4 7.5 convolution_bitcast_fusion.2
  556.0 3.9 convolution_bitcast_fusion
  559.9 3.9 convolution_bitcast_fusion.1
  565.1 24.8 %reduce-scatter.3.cloned.1.call-done = bf16[256,2048]{1,0:T(8,128)(2,1)} async-done(((bf16[1024,2048]{1,0:T(8,128)(2,1)}), bf16[256,2048]{1,0:T(8,128)(2,1)}) %reduce-scatter.3.cloned.1.call-update) | async-done | bytes 1048592 | tf_op jit(solution)/shard_map/reduce_scatter | solution.py:175
  589.8 2.8 convert_element_type.55
  592.7 41.2 %all-reduce = (f32[128]{0:T(128)}, f32[2,128]{1,0:T(2,128)}) all-reduce(f32[128]{0:T(128)S(1)} %add.360, f32[2,128]{1,0:T(2,128)S(1)} %maximum_add_fusion.1), channel_id=1, replica_groups=mesh['obj'=4,'plane'=4,'tile'=2] {'obj','plane','tile'}, use_global_device_ids=true, to_apply=%region_36.37 | all-reduce | flops 384 | bytes 3072 | tf_op jit(solution)/shard_map/psum | solution.py:184
  633.9 4.2 convolution_convert_fusion.2
  641.2 87.1 %all-reduce.11.cloned.1.call-done = f32[2,1152,128]{2,1,0:T(8,128)} async-done(((f32[2,1152,128]{2,1,0:T(8,128)}), f32[2,1152,128]{2,1,0:T(8,128)}) %all-reduce.11.cloned.1.call-update) | async-done | bytes 1179664 | tf_op jit(solution)/shard_map/psum | solution.py:184
  728.2 43.9 %reduce-scatter.5.cloned.1.call-done = f32[32,2048]{1,0:T(8,128)} async-done(((f32[256,2048]{1,0:T(8,128)}), f32[32,2048]{1,0:T(8,128)}) %reduce-scatter.5.cloned.1.call-update) | async-done | bytes 262160 | tf_op jit(solution)/shard_map/reduce_scatter | solution.py:183
  772.2 2.4 copy.157
  (370 shorter events, 159.2 us)
Async XLA Ops:
  7.2 107.7 %all-reduce.19.cloned.1.call-start = ((), (), s32[]{:S(2)}) async-start(), calls=%async_computation.8 | async-start | bytes 1572864 | tf_op jit(solution)/shard_map/psum | solution.py:86
  12.4 76.3 %copy-start.5 = (bf16[3,32,64,128]{3,2,1,0:T(8,128)(2,1)}, bf16[3,32,64,128]{3,2,1,0:T(8,128)(2,1)S(1)}, u32[]{:S(2)}) copy-start(bf16[3,32,64,128]{3,2,1,0:T(8,128)(2,1)S(1)} %get-tuple-element.53) | copy-start | bytes 4718596
  12.4 85.8 %copy-start.7 = (bf16[3,32,64,128]{3,2,1,0:T(8,128)(2,1)}, bf16[3,32,64,128]{3,2,1,0:T(8,128)(2,1)S(1)}, u32[]{:S(2)}) copy-start(bf16[3,32,64,128]{3,2,1,0:T(8,128)(2,1)S(1)} %get-tuple-element.52) | copy-start | bytes 4718596
  13.1 63.3 %collective-permute-start = (bf16[3,1,64,128]{3,2,1,0:T(8,128)(2,1)}, bf16[3,1,64,128]{3,2,1,0:T(8,128)(2,1)}, u32[]{:S(2)}, u32[]{:S(2)}) collective-permute-start(bf16[3,1,64,128]{3,2,1,0:T(8,128)(2,1)} %get-tuple-element.101), channel_id=1, source_target_pairs={{0,2},{2,4},{4,6},{1,3},{3,5},{5,7},{8,10},{10,12},{12,14},{9,11},... | collective-permute-start | bytes 147464 | tf_op jit(solution)/shard_map/ppermute | solution.py:14
  16.1 60.3 %collective-permute-start.1 = (bf16[3,1,64,128]{3,2,1,0:T(8,128)(2,1)}, bf16[3,1,64,128]{3,2,1,0:T(8,128)(2,1)}, u32[]{:S(2)}, u32[]{:S(2)}) collective-permute-start(bf16[3,1,64,128]{3,2,1,0:T(8,128)(2,1)} %get-tuple-element.102), channel_id=1, source_target_pairs={{2,0},{4,2},{6,4},{3,1},{5,3},{7,5},{10,8},{12,10},{14,12},{11,9},... | collective-permute-start | bytes 147464 | tf_op jit(solution)/shard_map/ppermute | solution.py:15
  18.0 52.8 %collective-permute-start.12 = (bf16[3,1,64,128]{3,2,1,0:T(8,128)(2,1)}, bf16[3,1,64,128]{3,2,1,0:T(8,128)(2,1)}, u32[]{:S(2)}, u32[]{:S(2)}) collective-permute-start(bf16[3,1,64,128]{3,2,1,0:T(8,128)(2,1)} %get-tuple-element.105), channel_id=1, source_target_pairs={{0,2},{2,4},{4,6},{1,3},{3,5},{5,7},{8,10},{10,12},{12,14},{9,11},... | collective-permute-start | bytes 147464 | tf_op jit(solution)/shard_map/ppermute | solution.py:14
  23.2 47.7 %collective-permute-start.13 = (bf16[3,1,64,128]{3,2,1,0:T(8,128)(2,1)}, bf16[3,1,64,128]{3,2,1,0:T(8,128)(2,1)}, u32[]{:S(2)}, u32[]{:S(2)}) collective-permute-start(bf16[3,1,64,128]{3,2,1,0:T(8,128)(2,1)} %get-tuple-element.106), channel_id=1, source_target_pairs={{2,0},{4,2},{6,4},{3,1},{5,3},{7,5},{10,8},{12,10},{14,12},{11,9},... | collective-permute-start | bytes 147464 | tf_op jit(solution)/shard_map/ppermute | solution.py:15
  49.5 10.2 %copy-start.56 = (f32[2,128]{1,0:T(2,128)S(1)}, f32[2,128]{1,0:T(2,128)}, u32[]{:S(2)}) copy-start(f32[2,128]{1,0:T(2,128)} %param.11) | copy-start | bytes 3076
  55.0 191.8 %all-reduce.17.cloned.1.call-start = ((), (), s32[]{:S(2)}) async-start(), calls=%async_computation.7 | async-start | bytes 1572864 | tf_op jit(solution)/shard_map/psum | solution.py:86
  71.7 11.8 %collective-permute-start.15 = (bf16[3,34,1,128]{3,2,1,0:T(2,128)(2,1)S(1)}, bf16[3,34,1,128]{3,2,1,0:T(2,128)(2,1)S(1)}, u32[]{:S(2)}, u32[]{:S(2)}) collective-permute-start(bf16[3,34,1,128]{3,2,1,0:T(2,128)(2,1)S(1)} %get-tuple-element.85), channel_id=1, source_target_pairs={{0,1},{2,3},{4,5},{6,7},{8,9},{10,11},{12,13},{14,15},{16,17},{18,... | collective-permute-start | bytes 78344 | tf_op jit(solution)/shard_map/ppermute | solution.py:14
  75.0 8.5 %collective-permute-start.14 = (bf16[3,34,1,128]{3,2,1,0:T(2,128)(2,1)S(1)}, bf16[3,34,1,128]{3,2,1,0:T(2,128)(2,1)S(1)}, u32[]{:S(2)}, u32[]{:S(2)}) collective-permute-start(bf16[3,34,1,128]{3,2,1,0:T(2,128)(2,1)S(1)} %get-tuple-element.86), channel_id=1, source_target_pairs={{1,0},{3,2},{5,4},{7,6},{9,8},{11,10},{13,12},{15,14},{17,16},{19,... | collective-permute-start | bytes 78344 | tf_op jit(solution)/shard_map/ppermute | solution.py:15
  77.2 17.2 %collective-permute-start.3 = (bf16[3,34,1,128]{3,2,1,0:T(2,128)(2,1)S(1)}, bf16[3,34,1,128]{3,2,1,0:T(2,128)(2,1)S(1)}, u32[]{:S(2)}, u32[]{:S(2)}) collective-permute-start(bf16[3,34,1,128]{3,2,1,0:T(2,128)(2,1)S(1)} %get-tuple-element.77), channel_id=1, source_target_pairs={{0,1},{2,3},{4,5},{6,7},{8,9},{10,11},{12,13},{14,15},{16,17},{18,... | collective-permute-start | bytes 78344 | tf_op jit(solution)/shard_map/ppermute | solution.py:14
  81.7 12.6 %collective-permute-start.2 = (bf16[3,34,1,128]{3,2,1,0:T(2,128)(2,1)S(1)}, bf16[3,34,1,128]{3,2,1,0:T(2,128)(2,1)S(1)}, u32[]{:S(2)}, u32[]{:S(2)}) collective-permute-start(bf16[3,34,1,128]{3,2,1,0:T(2,128)(2,1)S(1)} %get-tuple-element.78), channel_id=1, source_target_pairs={{1,0},{3,2},{5,4},{7,6},{9,8},{11,10},{13,12},{15,14},{17,16},{19,... | collective-permute-start | bytes 78344 | tf_op jit(solution)/shard_map/ppermute | solution.py:15
  86.8 20.4 %copy-start.19 = (bf16[3,34,65,128]{3,2,1,0:T(8,128)(2,1)}, bf16[3,34,65,128]{3,2,1,0:T(8,128)(2,1)S(1)}, u32[]{:S(2)}) copy-start(bf16[3,34,65,128]{3,2,1,0:T(8,128)(2,1)S(1)} %get-tuple-element.83) | copy-start | bytes 5091844
  122.8 10.8 %collective-permute-start.16 = (bf16[3,1,64,128]{3,2,1,0:T(8,128)(2,1)S(1)}, bf16[3,1,64,128]{3,2,1,0:T(8,128)(2,1)S(1)}, u32[]{:S(2)}, u32[]{:S(2)}) collective-permute-start(bf16[3,1,64,128]{3,2,1,0:T(8,128)(2,1)S(1)} %get-tuple-element.107), channel_id=1, source_target_pairs={{0,2},{2,4},{4,6},{1,3},{3,5},{5,7},{8,10},{10,12},{12,14},{9,11},... | collective-permute-start | bytes 147464 | tf_op jit(solution)/shard_map/ppermute | solution.py:14
  125.7 7.9 %collective-permute-start.17 = (bf16[3,1,64,128]{3,2,1,0:T(8,128)(2,1)S(1)}, bf16[3,1,64,128]{3,2,1,0:T(8,128)(2,1)S(1)}, u32[]{:S(2)}, u32[]{:S(2)}) collective-permute-start(bf16[3,1,64,128]{3,2,1,0:T(8,128)(2,1)S(1)} %get-tuple-element.108), channel_id=1, source_target_pairs={{2,0},{4,2},{6,4},{3,1},{5,3},{7,5},{10,8},{12,10},{14,12},{11,9},... | collective-permute-start | bytes 147464 | tf_op jit(solution)/shard_map/ppermute | solution.py:15
  127.0 12.6 %collective-permute-start.4 = (bf16[3,1,64,128]{3,2,1,0:T(8,128)(2,1)S(1)}, bf16[3,1,64,128]{3,2,1,0:T(8,128)(2,1)S(1)}, u32[]{:S(2)}, u32[]{:S(2)}) collective-permute-start(bf16[3,1,64,128]{3,2,1,0:T(8,128)(2,1)S(1)} %get-tuple-element.103), channel_id=1, source_target_pairs={{0,2},{2,4},{4,6},{1,3},{3,5},{5,7},{8,10},{10,12},{12,14},{9,11},... | collective-permute-start | bytes 147464 | tf_op jit(solution)/shard_map/ppermute | solution.py:14
  132.2 7.5 collective-permute-start.5
  133.8 11.8 %collective-permute-start.19 = (bf16[3,34,1,128]{3,2,1,0:T(2,128)(2,1)S(1)}, bf16[3,34,1,128]{3,2,1,0:T(2,128)(2,1)S(1)}, u32[]{:S(2)}, u32[]{:S(2)}) collective-permute-start(bf16[3,34,1,128]{3,2,1,0:T(2,128)(2,1)S(1)} %get-tuple-element.89), channel_id=1, source_target_pairs={{1,0},{3,2},{5,4},{7,6},{9,8},{11,10},{13,12},{15,14},{17,16},{19,... | collective-permute-start | bytes 78344 | tf_op jit(solution)/shard_map/ppermute | solution.py:15
  135.1 10.5 %collective-permute-start.18 = (bf16[3,34,1,128]{3,2,1,0:T(2,128)(2,1)S(1)}, bf16[3,34,1,128]{3,2,1,0:T(2,128)(2,1)S(1)}, u32[]{:S(2)}, u32[]{:S(2)}) collective-permute-start(bf16[3,34,1,128]{3,2,1,0:T(2,128)(2,1)S(1)} %get-tuple-element.90), channel_id=1, source_target_pairs={{0,1},{2,3},{4,5},{6,7},{8,9},{10,11},{12,13},{14,15},{16,17},{18,... | collective-permute-start | bytes 78344 | tf_op jit(solution)/shard_map/ppermute | solution.py:14
  139.7 13.5 %collective-permute-start.7 = (bf16[3,34,1,128]{3,2,1,0:T(2,128)(2,1)S(1)}, bf16[3,34,1,128]{3,2,1,0:T(2,128)(2,1)S(1)}, u32[]{:S(2)}, u32[]{:S(2)}) collective-permute-start(bf16[3,34,1,128]{3,2,1,0:T(2,128)(2,1)S(1)} %get-tuple-element.81), channel_id=1, source_target_pairs={{1,0},{3,2},{5,4},{7,6},{9,8},{11,10},{13,12},{15,14},{17,16},{19,... | collective-permute-start | bytes 78344 | tf_op jit(solution)/shard_map/ppermute | solution.py:15
  141.0 12.2 %collective-permute-start.6 = (bf16[3,34,1,128]{3,2,1,0:T(2,128)(2,1)S(1)}, bf16[3,34,1,128]{3,2,1,0:T(2,128)(2,1)S(1)}, u32[]{:S(2)}, u32[]{:S(2)}) collective-permute-start(bf16[3,34,1,128]{3,2,1,0:T(2,128)(2,1)S(1)} %get-tuple-element.82), channel_id=1, source_target_pairs={{0,1},{2,3},{4,5},{6,7},{8,9},{10,11},{12,13},{14,15},{16,17},{18,... | collective-permute-start | bytes 78344 | tf_op jit(solution)/shard_map/ppermute | solution.py:14
  153.2 17.5 %copy-start.20 = (bf16[3,32,64,1152]{3,2,1,0:T(8,128)(2,1)}, bf16[3,32,64,1152]{3,2,1,0:T(8,128)(2,1)S(1)}, u32[]{:S(2)}) copy-start(bf16[3,32,64,1152]{3,2,1,0:T(8,128)(2,1)S(1)} %slice_dynamic-update-slice_fusion.18) | copy-start | bytes 42467332
  188.0 158.0 %all-reduce.15.cloned.1.call-start = ((), (), s32[]{:S(2)}) async-start(), calls=%async_computation.6 | async-start | bytes 1572864 | tf_op jit(solution)/shard_map/psum | solution.py:86
  250.9 15.0 %copy-start.38 = (f32[3,32,128]{2,1,0:T(8,128)}, f32[3,32,128]{2,1,0:T(8,128)S(1)}, u32[]{:S(2)}) copy-start(f32[3,32,128]{2,1,0:T(8,128)S(1)} %fusion.61) | copy-start | bytes 147460
  253.6 40.5 %copy-start.1 = (bf16[3,32,64,128]{3,2,1,0:T(8,128)(2,1)}, bf16[3,32,64,128]{3,2,1,0:T(8,128)(2,1)S(1)}, u32[]{:S(2)}) copy-start(bf16[3,32,64,128]{3,2,1,0:T(8,128)(2,1)S(1)} %multiply_convert_fusion) | copy-start | bytes 4718596
  253.6 13.2 %slice-start.8 = ((s8[14155776]{0:T(1024)(128)(4,1)}), s8[4194304]{0:T(1024)(128)(4,1)S(1)}, s32[]{:S(2)}) async-start(s8[14155776]{0:T(1024)(128)(4,1)} %bitcast.178), calls=%async_computation.17 | async-start | bytes 8388608
  253.7 12.3 %copy-start.15 = (f32[3,32,64,128]{3,2,1,0:T(8,128)S(1)}, f32[3,32,64,128]{3,2,1,0:T(8,128)}, u32[]{:S(2)}) copy-start(f32[3,32,64,128]{3,2,1,0:T(8,128)} %get-tuple-element.163) | copy-start | bytes 9437188
  253.7 13.1 %slice-start.9 = ((s8[14155776]{0:T(1024)(128)(4,1)}), s8[4194304]{0:T(1024)(128)(4,1)S(1)}, s32[]{:S(2)}) async-start(s8[14155776]{0:T(1024)(128)(4,1)} %bitcast.178), calls=%async_computation.18 | async-start | bytes 8388608
  253.7 13.1 %slice-start.10 = ((s8[14155776]{0:T(1024)(128)(4,1)}), s8[4194304]{0:T(1024)(128)(4,1)S(1)}, s32[]{:S(2)}) async-start(s8[14155776]{0:T(1024)(128)(4,1)} %bitcast.178), calls=%async_computation.19 | async-start | bytes 8388608
  253.7 13.1 %slice-start.11 = ((s8[14155776]{0:T(1024)(128)(4,1)}), s8[1572864]{0:T(1024)(128)(4,1)S(1)}, s32[]{:S(2)}) async-start(s8[14155776]{0:T(1024)(128)(4,1)} %bitcast.178), calls=%async_computation.20 | async-start | bytes 3145728
  265.9 7.5 copy-start.40
  266.8 40.7 %copy-start.3 = (bf16[3,32,64,128]{3,2,1,0:T(8,128)(2,1)}, bf16[3,32,64,128]{3,2,1,0:T(8,128)(2,1)S(1)}, u32[]{:S(2)}) copy-start(bf16[3,32,64,128]{3,2,1,0:T(8,128)(2,1)S(1)} %multiply_convert_fusion.1) | copy-start | bytes 4718596
  274.0 13.4 %collective-permute-start.24 = (bf16[3,1,64,128]{3,2,1,0:T(8,128)(2,1)}, bf16[3,1,64,128]{3,2,1,0:T(8,128)(2,1)}, u32[]{:S(2)}, u32[]{:S(2)}) collective-permute-start(bf16[3,1,64,128]{3,2,1,0:T(8,128)(2,1)} %get-tuple-element.93), channel_id=1, source_target_pairs={{0,2},{2,4},{4,6},{1,3},{3,5},{5,7},{8,10},{10,12},{12,14},{9,11},... | collective-permute-start | bytes 147464 | tf_op jit(solution)/shard_map/ppermute | solution.py:14
  275.9 11.5 %collective-permute-start.25 = (bf16[3,1,64,128]{3,2,1,0:T(8,128)(2,1)}, bf16[3,1,64,128]{3,2,1,0:T(8,128)(2,1)}, u32[]{:S(2)}, u32[]{:S(2)}) collective-permute-start(bf16[3,1,64,128]{3,2,1,0:T(8,128)(2,1)} %get-tuple-element.94), channel_id=1, source_target_pairs={{2,0},{4,2},{6,4},{3,1},{5,3},{7,5},{10,8},{12,10},{14,12},{11,9},... | collective-permute-start | bytes 147464 | tf_op jit(solution)/shard_map/ppermute | solution.py:15
  277.9 16.3 %collective-permute-start.28 = (bf16[3,1,64,128]{3,2,1,0:T(8,128)(2,1)}, bf16[3,1,64,128]{3,2,1,0:T(8,128)(2,1)}, u32[]{:S(2)}, u32[]{:S(2)}) collective-permute-start(bf16[3,1,64,128]{3,2,1,0:T(8,128)(2,1)} %get-tuple-element.91), channel_id=1, source_target_pairs={{0,2},{2,4},{4,6},{1,3},{3,5},{5,7},{8,10},{10,12},{12,14},{9,11},... | collective-permute-start | bytes 147464 | tf_op jit(solution)/shard_map/ppermute | solution.py:14
  282.0 12.2 %collective-permute-start.29 = (bf16[3,1,64,128]{3,2,1,0:T(8,128)(2,1)}, bf16[3,1,64,128]{3,2,1,0:T(8,128)(2,1)}, u32[]{:S(2)}, u32[]{:S(2)}) collective-permute-start(bf16[3,1,64,128]{3,2,1,0:T(8,128)(2,1)} %get-tuple-element.92), channel_id=1, source_target_pairs={{2,0},{4,2},{6,4},{3,1},{5,3},{7,5},{10,8},{12,10},{14,12},{11,9},... | collective-permute-start | bytes 147464 | tf_op jit(solution)/shard_map/ppermute | solution.py:15
  287.4 194.0 %all-reduce.13.cloned.1.call-start = ((), (), s32[]{:S(2)}) async-start(), calls=%async_computation.5 | async-start | bytes 1572864 | tf_op jit(solution)/shard_map/psum | solution.py:86
  288.3 14.6 %collective-permute-start.27 = (bf16[3,34,1,128]{3,2,1,0:T(2,128)(2,1)S(1)}, bf16[3,34,1,128]{3,2,1,0:T(2,128)(2,1)S(1)}, u32[]{:S(2)}, u32[]{:S(2)}) collective-permute-start(bf16[3,34,1,128]{3,2,1,0:T(2,128)(2,1)S(1)} %get-tuple-element.65), channel_id=1, source_target_pairs={{1,0},{3,2},{5,4},{7,6},{9,8},{11,10},{13,12},{15,14},{17,16},{19,... | collective-permute-start | bytes 78344 | tf_op jit(solution)/shard_map/ppermute | solution.py:15
  289.6 13.3 %collective-permute-start.26 = (bf16[3,34,1,128]{3,2,1,0:T(2,128)(2,1)S(1)}, bf16[3,34,1,128]{3,2,1,0:T(2,128)(2,1)S(1)}, u32[]{:S(2)}, u32[]{:S(2)}) collective-permute-start(bf16[3,34,1,128]{3,2,1,0:T(2,128)(2,1)S(1)} %get-tuple-element.66), channel_id=1, source_target_pairs={{0,1},{2,3},{4,5},{6,7},{8,9},{10,11},{12,13},{14,15},{16,17},{18,... | collective-permute-start | bytes 78344 | tf_op jit(solution)/shard_map/ppermute | solution.py:14
  295.6 226.6 %collective-permute-start.31 = (bf16[3,34,1,128]{3,2,1,0:T(2,128)(2,1)}, bf16[3,34,1,128]{3,2,1,0:T(2,128)(2,1)}, u32[]{:S(2)}, u32[]{:S(2)}) collective-permute-start(bf16[3,34,1,128]{3,2,1,0:T(2,128)(2,1)} %get-tuple-element.61), channel_id=1, source_target_pairs={{1,0},{3,2},{5,4},{7,6},{9,8},{11,10},{13,12},{15,14},{17,16},{19,... | collective-permute-start | bytes 78344 | tf_op jit(solution)/shard_map/ppermute | solution.py:15
  297.1 225.1 %collective-permute-start.30 = (bf16[3,34,1,128]{3,2,1,0:T(2,128)(2,1)}, bf16[3,34,1,128]{3,2,1,0:T(2,128)(2,1)}, u32[]{:S(2)}, u32[]{:S(2)}) collective-permute-start(bf16[3,34,1,128]{3,2,1,0:T(2,128)(2,1)} %get-tuple-element.62), channel_id=1, source_target_pairs={{0,1},{2,3},{4,5},{6,7},{8,9},{10,11},{12,13},{14,15},{16,17},{18,... | collective-permute-start | bytes 78344 | tf_op jit(solution)/shard_map/ppermute | solution.py:14
  355.0 6.7 collective-permute-start.20
  356.3 6.7 collective-permute-start.21
  357.6 7.9 %collective-permute-start.8 = (bf16[3,1,64,128]{3,2,1,0:T(8,128)(2,1)S(1)}, bf16[3,1,64,128]{3,2,1,0:T(8,128)(2,1)S(1)}, u32[]{:S(2)}, u32[]{:S(2)}) collective-permute-start(bf16[3,1,64,128]{3,2,1,0:T(8,128)(2,1)S(1)} %get-tuple-element.97), channel_id=1, source_target_pairs={{0,2},{2,4},{4,6},{1,3},{3,5},{5,7},{8,10},{10,12},{12,14},{9,11},... | collective-permute-start | bytes 147464 | tf_op jit(solution)/shard_map/ppermute | solution.py:14
  361.7 5.1 collective-permute-start.9
  363.1 8.3 %collective-permute-start.23 = (bf16[3,34,1,128]{3,2,1,0:T(2,128)(2,1)S(1)}, bf16[3,34,1,128]{3,2,1,0:T(2,128)(2,1)S(1)}, u32[]{:S(2)}, u32[]{:S(2)}) collective-permute-start(bf16[3,34,1,128]{3,2,1,0:T(2,128)(2,1)S(1)} %get-tuple-element.73), channel_id=1, source_target_pairs={{0,1},{2,3},{4,5},{6,7},{8,9},{10,11},{12,13},{14,15},{16,17},{18,... | collective-permute-start | bytes 78344 | tf_op jit(solution)/shard_map/ppermute | solution.py:14
  365.5 7.3 collective-permute-start.22
  366.9 13.4 %collective-permute-start.11 = (bf16[3,34,1,128]{3,2,1,0:T(2,128)(2,1)S(1)}, bf16[3,34,1,128]{3,2,1,0:T(2,128)(2,1)S(1)}, u32[]{:S(2)}, u32[]{:S(2)}) collective-permute-start(bf16[3,34,1,128]{3,2,1,0:T(2,128)(2,1)S(1)} %get-tuple-element.69), channel_id=1, source_target_pairs={{0,1},{2,3},{4,5},{6,7},{8,9},{10,11},{12,13},{14,15},{16,17},{18,... | collective-permute-start | bytes 78344 | tf_op jit(solution)/shard_map/ppermute | solution.py:14
  371.5 8.8 %collective-permute-start.10 = (bf16[3,34,1,128]{3,2,1,0:T(2,128)(2,1)S(1)}, bf16[3,34,1,128]{3,2,1,0:T(2,128)(2,1)S(1)}, u32[]{:S(2)}, u32[]{:S(2)}) collective-permute-start(bf16[3,34,1,128]{3,2,1,0:T(2,128)(2,1)S(1)} %get-tuple-element.70), channel_id=1, source_target_pairs={{1,0},{3,2},{5,4},{7,6},{9,8},{11,10},{13,12},{15,14},{17,16},{19,... | collective-permute-start | bytes 78344 | tf_op jit(solution)/shard_map/ppermute | solution.py:15
  397.2 6.6 copy-start.10
  397.2 6.6 copy-start.46
  420.7 169.1 %reduce-scatter.3.cloned.1.call-start = ((), (), s32[]{:S(2)}) async-start(), calls=%async_computation.2 | async-start | bytes 5242880 | tf_op jit(solution)/shard_map/reduce_scatter | solution.py:175
  513.5 214.7 %all-reduce.11.cloned.1.call-start = ((), (), s32[]{:S(2)}) async-start(), calls=%async_computation.4 | async-start | bytes 2359296 | tf_op jit(solution)/shard_map/psum | solution.py:184
  532.9 8.1 %copy-start.27 = (bf16[1,3,32,64,128]{4,3,2,1,0:T(8,128)(2,1)S(1)}, bf16[1,3,32,64,128]{4,3,2,1,0:T(8,128)(2,1)}, u32[]{:S(2)}) copy-start(bf16[1,3,32,64,128]{4,3,2,1,0:T(8,128)(2,1)} %get-tuple-element.54) | copy-start | bytes 4718596
  541.0 7.3 copy-start.26
  541.0 14.9 %slice-start = ((s8[14155776]{0:T(1024)(128)(4,1)}), s8[4194304]{0:T(1024)(128)(4,1)S(1)}, s32[]{:S(2)}) async-start(s8[14155776]{0:T(1024)(128)(4,1)} %bitcast.154), calls=%async_computation.9 | async-start | bytes 8388608
  541.0 14.9 %slice-start.1 = ((s8[14155776]{0:T(1024)(128)(4,1)}), s8[4194304]{0:T(1024)(128)(4,1)S(1)}, s32[]{:S(2)}) async-start(s8[14155776]{0:T(1024)(128)(4,1)} %bitcast.154), calls=%async_computation.10 | async-start | bytes 8388608
  548.3 7.6 slice-start.2
  548.4 7.6 slice-start.3
  548.4 11.5 %slice-start.4 = ((s8[14155776]{0:T(1024)(128)(4,1)}), s8[4194304]{0:T(1024)(128)(4,1)S(1)}, s32[]{:S(2)}) async-start(s8[14155776]{0:T(1024)(128)(4,1)} %bitcast.156), calls=%async_computation.13 | async-start | bytes 8388608
  548.4 11.5 %slice-start.5 = ((s8[14155776]{0:T(1024)(128)(4,1)}), s8[4194304]{0:T(1024)(128)(4,1)S(1)}, s32[]{:S(2)}) async-start(s8[14155776]{0:T(1024)(128)(4,1)} %bitcast.156), calls=%async_computation.14 | async-start | bytes 8388608
  565.0 68.9 %copy-start.29 = (bf16[384,2048]{1,0:T(8,128)(2,1)S(1)}, bf16[384,2048]{1,0:T(8,128)(2,1)}, u32[]{:S(2)}) copy-start(bf16[384,2048]{1,0:T(8,128)(2,1)} %reshape.166) | copy-start | bytes 4718596
  565.0 207.1 %reduce-scatter.5.cloned.1.call-start = ((), (), s32[]{:S(2)}) async-start(), calls=%async_computation.3 | async-start | bytes 2359296 | tf_op jit(solution)/shard_map/reduce_scatter | solution.py:183
  (44 other events, 161.9 us)
Sparse Core Ops, SparseCore 0:
  55.1 59.0 all-reduce.18
  188.1 58.6 all-reduce.16
  287.5 58.4 all-reduce.14
  420.9 60.4 all-reduce.12
  513.6 76.1 reduce-scatter.2
  595.6 132.5 all-reduce.10
  732.1 40.0 reduce-scatter.4
where the time goes:
time: 792 us; the launch traced here: 782 us
  waiting for transfers between devices  298 us (38%)
  local copies, waits for them, and re-layouts  158 us (20%)
  matrix products  98 us (12%)
  other arithmetic  85.8 us (11%)
  starting transfers between devices  84.3 us (11%)
  blocking collectives  41.2 us (5%)
  between operations  16.3 us (2%)
    psum x4, waiting for transfers between devices, pooled_sums(): result = lax.psum((row_full, col_full), ('plane', 'tile'))  142 us
    psum x1, waiting for transfers between devices, per_device(): lax.psum((kernel_sum, conv_bias_sum, bias_grad), ('obj', 'plane', 'tile'))  87.1 us
    unnamed x184, local copies, waits for them, and re-layouts  71.6 us
    ppermute x16, starting transfers between devices, padded_2(): before = lax.ppermute(last, axis, up)  61.8 us
    dot_general x6, matrix products, convolve(): jnp.dot(gathered.reshape(-1, gathered.shape[-1]), kernel, preferred_eleme...  53.3 us
    reduce_scatter x1, waiting for transfers between devices, per_device(): lax.psum_scatter(object_part, ('plane', 'tile'), scatter_dimension=0, til...  43.9 us
    psum x1, blocking collectives, per_device(): lax.psum((kernel_sum, conv_bias_sum, bias_grad), ('obj', 'plane', 'tile'))  41.2 us
    concatenate x16, other arithmetic, padded_2(): array = jnp.concatenate([before, array, after], axis=dim)  26.6 us
  transfers between devices with their start and end apart: 39, of which 6 were waited for; matrix products, arithmetic and copies ran while one was open for 32% of the time, Pallas kernels for 0%

commit v1 on v0

--- a/solution.py
+++ b/solution.py
@@ -1,7 +1,17 @@
+import functools
 import jax
 import jax.numpy as jnp
 from jax import lax
 from jax.sharding import PartitionSpec as P
+
+
+def form_the_surface(xx, axis_key, axis_tag):
+    for s in (axis_key, axis_tag):
+        xx = lax.psum(xx, s)
+    return xx
+
+
+detail_the_sections = functools.partial(form_the_surface, axis_key="tile", axis_tag="plane")
 
 
 def padded_2(array, sides, width):
@@ -83,7 +93,7 @@
         col_part,
         (zero_index, col_start, zero_index),
     )
-    result = lax.psum((row_full, col_full), ("plane", "tile"))
+    result = detail_the_sections((row_full, col_full))
     return result
 
 

time: 792 us -> 867 us (1.095)
  waiting for transfers between devices: 298 us -> 367 us
    psum x4 -> x8, waiting for transfers between devices: 142 us -> 209 us  [form_the_surface(): xx = lax.psum(xx, s)]
    unnamed x184 -> x194, local copies, waits for them, and re-layouts: 71.6 us -> 76.5 us
  transfers between devices with their start and end apart: 39 -> 43, of which waited for: 6 -> 10; matrix products, arithmetic and copies ran while one was open for 32% -> 32% of each run, Pallas kernels for 0% -> 0%
where the time goes in v1:
time: 867 us; the launch traced here: 857 us
  waiting for transfers between devices  367 us (42%)
  local copies, waits for them, and re-layouts  165 us (19%)
  matrix products  97.8 us (11%)
  other arithmetic  88.2 us (10%)
  starting transfers between devices  81.9 us (9%)
  blocking collectives  41.1 us (5%)
  between operations  16 us (2%)
    psum x8, waiting for transfers between devices, form_the_surface(): xx = lax.psum(xx, s)  209 us
    psum x1, waiting for transfers between devices, per_device(): lax.psum((kernel_sum, conv_bias_sum, bias_grad), ('obj', 'plane', 'tile'))  87.3 us
    unnamed x194, local copies, waits for them, and re-layouts  76.5 us
    ppermute x16, starting transfers between devices, padded_2(): before = lax.ppermute(last, axis, up)  59.4 us
    dot_general x6, matrix products, convolve(): jnp.dot(gathered.reshape(-1, gathered.shape[-1]), kernel, preferred_eleme...  52.9 us
    reduce_scatter x1, waiting for transfers between devices, per_device(): lax.psum_scatter(object_part, ('plane', 'tile'), scatter_dimension=0, til...  43.9 us
    psum x1, blocking collectives, per_device(): lax.psum((kernel_sum, conv_bias_sum, bias_grad), ('obj', 'plane', 'tile'))  41.1 us
    concatenate x16, other arithmetic, padded_2(): array = jnp.concatenate([before, array, after], axis=dim)  27.8 us
  transfers between devices with their start and end apart: 43, of which 10 were waited for; matrix products, arithmetic and copies ran while one was open for 32% of the time, Pallas kernels for 0%

profile of v1, /device:TPU:0, one launch (start us, length us, event | category | flops | bytes accessed | tf_op | source)
XLA Modules:
  0.0 857.0 jit_solution(18420707119972364316)
XLA Ops:
  7.2 5.2 fusion.89
  13.0 3.0 collective-permute-start
  18.0 5.2 collective-permute-start.12
  24.4 7.7 dot_general.56
  32.1 7.5 copy.45
  39.7 4.0 convolution_bitcast_fusion.4
  43.8 4.4 add_reduce_fusion.2
  55.1 2.9 fusion.92
  59.8 3.2 copy.40
  65.8 5.1 copy.35
  71.7 3.3 collective-permute-start.15
  77.2 4.5 collective-permute-start.3
  83.6 3.3 maximum_maximum_fusion.3
  90.2 3.3 maximum_maximum_fusion
  103.2 5.0 copy-done.58
  109.8 3.4 slice_dynamic-update-slice_fusion.43
  115.4 33.8 %all-reduce.27.cloned.1.call-done = (f32[3,128,128]{2,1,0:T(8,128)}, f32[3,128,128]{2,1,0:T(8,128)}, f32[3,128,128]{2,1,0:T(8,128)}, f32[3,128,128]{2,1,0:T(8,128)}) async-done(((f32[3,128,128]{2,1,0:T(8,128)}, f32[3,128,128]{2,1,0:T(8,128)}, f32[3,128,128]{2,1,0:T(8,128)}, f32[3,128,128]{2,1,0:T(8,128)}), (f32[3,128,128]{2,1,0:T(8,128)}, f32[3,128,128]{2,1,0:T(8,128)}, f32[3,128,128]{2,1,0:T(8,128)}, ...) | async-done | bytes 786448 | tf_op jit(solution)/shard_map/psum | solution.py:10
  153.4 3.4 multiply_convert_fusion.3
  159.4 3.7 collective-permute-start.4
  165.9 4.5 collective-permute-start.18
  171.9 4.7 collective-permute-start.6
  202.1 5.7 fusion.88
  207.8 10.8 %fusion.85 = (f32[3,64,128]{2,1,0:T(8,128)S(1)}, f32[3,32,128]{2,1,0:T(8,128)S(1)}, f32[3,32,64,128]{3,2,1,0:T(8,128)}) fusion(f32[128]{0:T(128)S(1)} %slice_bitcast_fusion, bf16[3,32,64,1152]{3,2,1,0:T(8,128)(2,1)} %slice_dynamic-update-slice_fusion.36, bf16[2,1152,128]{2,1,0:T(8,128)(2,1)S(1)} %copy-done.27, f32[3,32,64,128]{3,2,1,0:T(8,128)S(1)} %bitcast.149, ...), kind=kOutput, calls=%fused_computation.314 | convolution fusion | flops 1815834624 | bytes 20890624 | tf_op jit(solution)/shard_map/dot_general | solution.py:42
  223.9 2.9 slice_dynamic-update-slice_fusion.42
  230.3 30.7 %all-reduce.33.cloned.1.call-done = (f32[3,128,128]{2,1,0:T(8,128)}, f32[3,128,128]{2,1,0:T(8,128)}, f32[3,128,128]{2,1,0:T(8,128)}, f32[3,128,128]{2,1,0:T(8,128)}) async-done(((f32[3,128,128]{2,1,0:T(8,128)}, f32[3,128,128]{2,1,0:T(8,128)}, f32[3,128,128]{2,1,0:T(8,128)}, f32[3,128,128]{2,1,0:T(8,128)}), (f32[3,128,128]{2,1,0:T(8,128)}, f32[3,128,128]{2,1,0:T(8,128)}, f32[3,128,128]{2,1,0:T(8,128)}, ...) | async-done | bytes 786448 | tf_op jit(solution)/shard_map/psum | solution.py:10
  265.1 33.3 %all-reduce.25.cloned.1.call-done = (f32[3,128,128]{2,1,0:T(8,128)}, f32[3,128,128]{2,1,0:T(8,128)}, f32[3,128,128]{2,1,0:T(8,128)}, f32[3,128,128]{2,1,0:T(8,128)}) async-done(((f32[3,128,128]{2,1,0:T(8,128)}, f32[3,128,128]{2,1,0:T(8,128)}, f32[3,128,128]{2,1,0:T(8,128)}, f32[3,128,128]{2,1,0:T(8,128)}), (f32[3,128,128]{2,1,0:T(8,128)}, f32[3,128,128]{2,1,0:T(8,128)}, f32[3,128,128]{2,1,0:T(8,128)}, ...) | async-done | bytes 786448 | tf_op jit(solution)/shard_map/psum | solution.py:10
  302.5 2.9 multiply_convert_fusion.1
  309.4 11.7 %fusion.84 = (f32[3,64,128]{2,1,0:T(8,128)S(1)}, f32[3,32,128]{2,1,0:T(8,128)S(1)}, f32[3,32,64,128]{3,2,1,0:T(8,128)}) fusion(f32[3,64,128]{2,1,0:T(8,128)S(1)} %fusion.51, f32[3,32,64,128]{3,2,1,0:T(8,128)S(1)} %copy-done.12, f32[3,32,128]{2,1,0:T(8,128)S(1)} %fusion.71, bf16[3,32,64,1152]{3,2,1,0:T(8,128)(2,1)} %slice_dynamic-update-slice_fusion.42, ...), kind=kOutput, calls=%fused_computation.313 | convolution fusion | flops 1821339648 | bytes 21037056 | tf_op jit(solution)/shard_map/dot_general | solution.py:42
  321.1 6.5 fusion.87
  332.1 3.1 collective-permute-start.28
  339.3 5.2 collective-permute-start.26
  344.4 22.2 %all-reduce.31.cloned.1.call-done = (f32[3,128,128]{2,1,0:T(8,128)}, f32[3,128,128]{2,1,0:T(8,128)}, f32[3,128,128]{2,1,0:T(8,128)}, f32[3,128,128]{2,1,0:T(8,128)}) async-done(((f32[3,128,128]{2,1,0:T(8,128)}, f32[3,128,128]{2,1,0:T(8,128)}, f32[3,128,128]{2,1,0:T(8,128)}, f32[3,128,128]{2,1,0:T(8,128)}), (f32[3,128,128]{2,1,0:T(8,128)}, f32[3,128,128]{2,1,0:T(8,128)}, f32[3,128,128]{2,1,0:T(8,128)}, ...) | async-done | bytes 786448 | tf_op jit(solution)/shard_map/psum | solution.py:10
  369.0 5.8 collective-permute-start.30
  374.8 4.4 pad_maximum_fusion.6
  379.2 24.9 %all-reduce.23.cloned.1.call-done = (f32[3,128,128]{2,1,0:T(8,128)}, f32[3,128,128]{2,1,0:T(8,128)}, f32[3,128,128]{2,1,0:T(8,128)}, f32[3,128,128]{2,1,0:T(8,128)}) async-done(((f32[3,128,128]{2,1,0:T(8,128)}, f32[3,128,128]{2,1,0:T(8,128)}, f32[3,128,128]{2,1,0:T(8,128)}, f32[3,128,128]{2,1,0:T(8,128)}), (f32[3,128,128]{2,1,0:T(8,128)}, f32[3,128,128]{2,1,0:T(8,128)}, f32[3,128,128]{2,1,0:T(8,128)}, ...) | async-done | bytes 786448 | tf_op jit(solution)/shard_map/psum | solution.py:10
  407.9 5.2 fusion.82
  415.8 3.7 collective-permute-start.8
  420.9 3.5 collective-permute-start.23
  425.8 4.5 collective-permute-start.11
  456.0 6.6 fusion.86
  462.7 11.7 %fusion.83 = (f32[3,64,128]{2,1,0:T(8,128)S(1)}, f32[3,32,128]{2,1,0:T(8,128)S(1)}, f32[3,32,64,128]{3,2,1,0:T(8,128)}) fusion(f32[3,64,128]{2,1,0:T(8,128)S(1)} %copy-done.51, f32[3,32,128]{2,1,0:T(8,128)S(1)} %copy-done.57, f32[3,32,64,128]{3,2,1,0:T(8,128)S(1)} %bitcast.150, f32[128]{0:T(128)S(1)} %copy-done.60, ...), kind=kOutput, calls=%fused_computation.312 | convolution fusion | flops 1822126080 | bytes 21037568 | tf_op jit(solution)/shard_map/dot_general | solution.py:42
  480.1 3.0 slice_dynamic-update-slice_fusion.11
  488.8 30.1 %all-reduce.29.cloned.1.call-done = (f32[3,128,128]{2,1,0:T(8,128)}, f32[3,128,128]{2,1,0:T(8,128)}, f32[3,128,128]{2,1,0:T(8,128)}, f32[3,128,128]{2,1,0:T(8,128)}) async-done(((f32[3,128,128]{2,1,0:T(8,128)}, f32[3,128,128]{2,1,0:T(8,128)}, f32[3,128,128]{2,1,0:T(8,128)}, f32[3,128,128]{2,1,0:T(8,128)}), (f32[3,128,128]{2,1,0:T(8,128)}, f32[3,128,128]{2,1,0:T(8,128)}, f32[3,128,128]{2,1,0:T(8,128)}, ...) | async-done | bytes 786448 | tf_op jit(solution)/shard_map/psum | solution.py:10
  518.9 3.9 constant_dynamic-update-slice_fusion.6
  522.8 33.6 %all-reduce.21.cloned.1.call-done = (f32[3,128,128]{2,1,0:T(8,128)}, f32[3,128,128]{2,1,0:T(8,128)}, f32[3,128,128]{2,1,0:T(8,128)}, f32[3,128,128]{2,1,0:T(8,128)}) async-done(((f32[3,128,128]{2,1,0:T(8,128)}, f32[3,128,128]{2,1,0:T(8,128)}, f32[3,128,128]{2,1,0:T(8,128)}, f32[3,128,128]{2,1,0:T(8,128)}), (f32[3,128,128]{2,1,0:T(8,128)}, f32[3,128,128]{2,1,0:T(8,128)}, f32[3,128,128]{2,1,0:T(8,128)}, ...) | async-done | bytes 786448 | tf_op jit(solution)/shard_map/psum | solution.py:10
  560.1 7.8 fusion.79
  569.9 3.8 reshape.166
  573.7 3.2 copy.58
  576.9 3.8 reshape.169
  580.7 7.8 convolution_convert_fusion
  588.6 3.6 slice_dynamic-update-slice_fusion.8
  592.2 2.9 slice_dynamic-update-slice_fusion.7
  597.3 3.1 pad_maximum_fusion.7
  609.7 5.0 copy-done.59
  614.7 7.3 convolution_bitcast_fusion.3
  622.1 7.6 convolution_bitcast_fusion.2
  629.8 3.9 convolution_bitcast_fusion
  633.8 3.9 convolution_bitcast_fusion.1
  638.9 26.6 %reduce-scatter.3.cloned.1.call-done = bf16[256,2048]{1,0:T(8,128)(2,1)} async-done(((bf16[1024,2048]{1,0:T(8,128)(2,1)}), bf16[256,2048]{1,0:T(8,128)(2,1)}) %reduce-scatter.3.cloned.1.call-update) | async-done | bytes 1048592 | tf_op jit(solution)/shard_map/reduce_scatter | solution.py:185
  665.5 2.8 convert_element_type.55
  668.3 41.1 %all-reduce = (f32[128]{0:T(128)}, f32[2,128]{1,0:T(2,128)}) all-reduce(f32[128]{0:T(128)S(1)} %add.392, f32[2,128]{1,0:T(2,128)S(1)} %maximum_add_fusion.1), channel_id=1, replica_groups=mesh['obj'=4,'plane'=4,'tile'=2] {'obj','plane','tile'}, use_global_device_ids=true, to_apply=%region_52.53 | all-reduce | flops 384 | bytes 3072 | tf_op jit(solution)/shard_map/psum | solution.py:194
  709.4 4.2 convolution_convert_fusion.2
  716.7 87.3 %all-reduce.19.cloned.1.call-done = f32[2,1152,128]{2,1,0:T(8,128)} async-done(((f32[2,1152,128]{2,1,0:T(8,128)}), f32[2,1152,128]{2,1,0:T(8,128)}) %all-reduce.19.cloned.1.call-update) | async-done | bytes 1179664 | tf_op jit(solution)/shard_map/psum | solution.py:194
  804.0 43.9 %reduce-scatter.5.cloned.1.call-done = f32[32,2048]{1,0:T(8,128)} async-done(((f32[256,2048]{1,0:T(8,128)}), f32[32,2048]{1,0:T(8,128)}) %reduce-scatter.5.cloned.1.call-update) | async-done | bytes 262160 | tf_op jit(solution)/shard_map/reduce_scatter | solution.py:193
  (392 shorter events, 174.3 us)
Async XLA Ops:
  7.2 102.6 %all-reduce.35.cloned.1.call-start = ((), (), s32[]{:S(2)}) async-start(), calls=%async_computation.12 | async-start | bytes 1572864 | tf_op jit(solution)/shard_map/psum | solution.py:10
  13.0 63.4 %collective-permute-start = (bf16[3,1,64,128]{3,2,1,0:T(8,128)(2,1)}, bf16[3,1,64,128]{3,2,1,0:T(8,128)(2,1)}, u32[]{:S(2)}, u32[]{:S(2)}) collective-permute-start(bf16[3,1,64,128]{3,2,1,0:T(8,128)(2,1)} %get-tuple-element.117), channel_id=1, source_target_pairs={{0,2},{2,4},{4,6},{1,3},{3,5},{5,7},{8,10},{10,12},{12,14},{9,11},... | collective-permute-start | bytes 147464 | tf_op jit(solution)/shard_map/ppermute | solution.py:24
  16.0 60.4 %collective-permute-start.1 = (bf16[3,1,64,128]{3,2,1,0:T(8,128)(2,1)}, bf16[3,1,64,128]{3,2,1,0:T(8,128)(2,1)}, u32[]{:S(2)}, u32[]{:S(2)}) collective-permute-start(bf16[3,1,64,128]{3,2,1,0:T(8,128)(2,1)} %get-tuple-element.118), channel_id=1, source_target_pairs={{2,0},{4,2},{6,4},{3,1},{5,3},{7,5},{10,8},{12,10},{14,12},{11,9},... | collective-permute-start | bytes 147464 | tf_op jit(solution)/shard_map/ppermute | solution.py:25
  18.0 52.9 %collective-permute-start.12 = (bf16[3,1,64,128]{3,2,1,0:T(8,128)(2,1)}, bf16[3,1,64,128]{3,2,1,0:T(8,128)(2,1)}, u32[]{:S(2)}, u32[]{:S(2)}) collective-permute-start(bf16[3,1,64,128]{3,2,1,0:T(8,128)(2,1)} %get-tuple-element.121), channel_id=1, source_target_pairs={{0,2},{2,4},{4,6},{1,3},{3,5},{5,7},{8,10},{10,12},{12,14},{9,11},... | collective-permute-start | bytes 147464 | tf_op jit(solution)/shard_map/ppermute | solution.py:24
  23.1 47.8 %collective-permute-start.13 = (bf16[3,1,64,128]{3,2,1,0:T(8,128)(2,1)}, bf16[3,1,64,128]{3,2,1,0:T(8,128)(2,1)}, u32[]{:S(2)}, u32[]{:S(2)}) collective-permute-start(bf16[3,1,64,128]{3,2,1,0:T(8,128)(2,1)} %get-tuple-element.122), channel_id=1, source_target_pairs={{2,0},{4,2},{6,4},{3,1},{5,3},{7,5},{10,8},{12,10},{14,12},{11,9},... | collective-permute-start | bytes 147464 | tf_op jit(solution)/shard_map/ppermute | solution.py:25
  49.6 10.2 %copy-start.61 = (f32[2,128]{1,0:T(2,128)S(1)}, f32[2,128]{1,0:T(2,128)}, u32[]{:S(2)}) copy-start(f32[2,128]{1,0:T(2,128)} %param.11) | copy-start | bytes 3076
  55.0 94.2 %all-reduce.27.cloned.1.call-start = ((), (), s32[]{:S(2)}) async-start(), calls=%async_computation.8 | async-start | bytes 1572864 | tf_op jit(solution)/shard_map/psum | solution.py:10
  71.7 11.8 %collective-permute-start.15 = (bf16[3,34,1,128]{3,2,1,0:T(2,128)(2,1)S(1)}, bf16[3,34,1,128]{3,2,1,0:T(2,128)(2,1)S(1)}, u32[]{:S(2)}, u32[]{:S(2)}) collective-permute-start(bf16[3,34,1,128]{3,2,1,0:T(2,128)(2,1)S(1)} %get-tuple-element.101), channel_id=1, source_target_pairs={{0,1},{2,3},{4,5},{6,7},{8,9},{10,11},{12,13},{14,15},{16,17},{18,... | collective-permute-start | bytes 78344 | tf_op jit(solution)/shard_map/ppermute | solution.py:24
  75.1 8.5 collective-permute-start.14
  77.2 12.9 %collective-permute-start.3 = (bf16[3,34,1,128]{3,2,1,0:T(2,128)(2,1)S(1)}, bf16[3,34,1,128]{3,2,1,0:T(2,128)(2,1)S(1)}, u32[]{:S(2)}, u32[]{:S(2)}) collective-permute-start(bf16[3,34,1,128]{3,2,1,0:T(2,128)(2,1)S(1)} %get-tuple-element.93), channel_id=1, source_target_pairs={{0,1},{2,3},{4,5},{6,7},{8,9},{10,11},{12,13},{14,15},{16,17},{18,... | collective-permute-start | bytes 78344 | tf_op jit(solution)/shard_map/ppermute | solution.py:24
  81.8 8.4 collective-permute-start.2
  93.5 14.7 %copy-start.20 = (bf16[3,34,65,128]{3,2,1,0:T(8,128)(2,1)}, bf16[3,34,65,128]{3,2,1,0:T(8,128)(2,1)S(1)}, u32[]{:S(2)}) copy-start(bf16[3,34,65,128]{3,2,1,0:T(8,128)(2,1)S(1)} %get-tuple-element.91) | copy-start | bytes 5091844
  109.8 151.2 %all-reduce.33.cloned.1.call-start = ((), (), s32[]{:S(2)}) async-start(), calls=%async_computation.11 | async-start | bytes 1572864 | tf_op jit(solution)/shard_map/psum | solution.py:10
  156.8 7.7 collective-permute-start.16
  158.1 6.4 collective-permute-start.17
  159.4 11.0 %collective-permute-start.4 = (bf16[3,1,64,128]{3,2,1,0:T(8,128)(2,1)S(1)}, bf16[3,1,64,128]{3,2,1,0:T(8,128)(2,1)S(1)}, u32[]{:S(2)}, u32[]{:S(2)}) collective-permute-start(bf16[3,1,64,128]{3,2,1,0:T(8,128)(2,1)S(1)} %get-tuple-element.119), channel_id=1, source_target_pairs={{0,2},{2,4},{4,6},{1,3},{3,5},{5,7},{8,10},{10,12},{12,14},{9,11},... | collective-permute-start | bytes 147464 | tf_op jit(solution)/shard_map/ppermute | solution.py:24
  163.2 7.3 collective-permute-start.5
  164.6 12.0 %collective-permute-start.19 = (bf16[3,34,1,128]{3,2,1,0:T(2,128)(2,1)S(1)}, bf16[3,34,1,128]{3,2,1,0:T(2,128)(2,1)S(1)}, u32[]{:S(2)}, u32[]{:S(2)}) collective-permute-start(bf16[3,34,1,128]{3,2,1,0:T(2,128)(2,1)S(1)} %get-tuple-element.105), channel_id=1, source_target_pairs={{1,0},{3,2},{5,4},{7,6},{9,8},{11,10},{13,12},{15,14},{17,16},{19,... | collective-permute-start | bytes 78344 | tf_op jit(solution)/shard_map/ppermute | solution.py:25
  165.9 10.7 %collective-permute-start.18 = (bf16[3,34,1,128]{3,2,1,0:T(2,128)(2,1)S(1)}, bf16[3,34,1,128]{3,2,1,0:T(2,128)(2,1)S(1)}, u32[]{:S(2)}, u32[]{:S(2)}) collective-permute-start(bf16[3,34,1,128]{3,2,1,0:T(2,128)(2,1)S(1)} %get-tuple-element.106), channel_id=1, source_target_pairs={{0,1},{2,3},{4,5},{6,7},{8,9},{10,11},{12,13},{14,15},{16,17},{18,... | collective-permute-start | bytes 78344 | tf_op jit(solution)/shard_map/ppermute | solution.py:24
  170.6 13.7 %collective-permute-start.7 = (bf16[3,34,1,128]{3,2,1,0:T(2,128)(2,1)S(1)}, bf16[3,34,1,128]{3,2,1,0:T(2,128)(2,1)S(1)}, u32[]{:S(2)}, u32[]{:S(2)}) collective-permute-start(bf16[3,34,1,128]{3,2,1,0:T(2,128)(2,1)S(1)} %get-tuple-element.97), channel_id=1, source_target_pairs={{1,0},{3,2},{5,4},{7,6},{9,8},{11,10},{13,12},{15,14},{17,16},{19,... | collective-permute-start | bytes 78344 | tf_op jit(solution)/shard_map/ppermute | solution.py:25
  171.9 12.4 %collective-permute-start.6 = (bf16[3,34,1,128]{3,2,1,0:T(2,128)(2,1)S(1)}, bf16[3,34,1,128]{3,2,1,0:T(2,128)(2,1)S(1)}, u32[]{:S(2)}, u32[]{:S(2)}) collective-permute-start(bf16[3,34,1,128]{3,2,1,0:T(2,128)(2,1)S(1)} %get-tuple-element.98), channel_id=1, source_target_pairs={{0,1},{2,3},{4,5},{6,7},{8,9},{10,11},{12,13},{14,15},{16,17},{18,... | collective-permute-start | bytes 78344 | tf_op jit(solution)/shard_map/ppermute | solution.py:24
  184.2 17.8 %copy-start.22 = (bf16[3,32,64,1152]{3,2,1,0:T(8,128)(2,1)}, bf16[3,32,64,1152]{3,2,1,0:T(8,128)(2,1)S(1)}, u32[]{:S(2)}) copy-start(bf16[3,32,64,1152]{3,2,1,0:T(8,128)(2,1)S(1)} %slice_dynamic-update-slice_fusion.18) | copy-start | bytes 42467332
  218.5 8.3 copy-start.17
  223.8 74.6 %all-reduce.25.cloned.1.call-start = ((), (), s32[]{:S(2)}) async-start(), calls=%async_computation.7 | async-start | bytes 1572864 | tf_op jit(solution)/shard_map/psum | solution.py:10
  261.0 105.7 %all-reduce.31.cloned.1.call-start = ((), (), s32[]{:S(2)}) async-start(), calls=%async_computation.10 | async-start | bytes 1572864 | tf_op jit(solution)/shard_map/psum | solution.py:10
  301.3 8.0 copy-start.12
  302.5 18.6 %copy-start.41 = (f32[3,32,128]{2,1,0:T(8,128)}, f32[3,32,128]{2,1,0:T(8,128)S(1)}, u32[]{:S(2)}) copy-start(f32[3,32,128]{2,1,0:T(8,128)S(1)} %fusion.71) | copy-start | bytes 147460
  302.5 18.6 %slice-start.8 = ((s8[14155776]{0:T(1024)(128)(4,1)}), s8[4194304]{0:T(1024)(128)(4,1)S(1)}, s32[]{:S(2)}) async-start(s8[14155776]{0:T(1024)(128)(4,1)} %bitcast.178), calls=%async_computation.21 | async-start | bytes 8388608
  305.4 69.4 %copy-start.1 = (bf16[3,32,64,128]{3,2,1,0:T(8,128)(2,1)}, bf16[3,32,64,128]{3,2,1,0:T(8,128)(2,1)S(1)}, u32[]{:S(2)}) copy-start(bf16[3,32,64,128]{3,2,1,0:T(8,128)(2,1)S(1)} %multiply_convert_fusion.1) | copy-start | bytes 4718596
  306.1 30.4 %collective-permute-start.24 = (bf16[3,1,64,128]{3,2,1,0:T(8,128)(2,1)}, bf16[3,1,64,128]{3,2,1,0:T(8,128)(2,1)}, u32[]{:S(2)}, u32[]{:S(2)}) collective-permute-start(bf16[3,1,64,128]{3,2,1,0:T(8,128)(2,1)} %get-tuple-element.109), channel_id=1, source_target_pairs={{0,2},{2,4},{4,6},{1,3},{3,5},{5,7},{8,10},{10,12},{12,14},{9,11},... | collective-permute-start | bytes 147464 | tf_op jit(solution)/shard_map/ppermute | solution.py:24
  308.0 28.5 %collective-permute-start.25 = (bf16[3,1,64,128]{3,2,1,0:T(8,128)(2,1)}, bf16[3,1,64,128]{3,2,1,0:T(8,128)(2,1)}, u32[]{:S(2)}, u32[]{:S(2)}) collective-permute-start(bf16[3,1,64,128]{3,2,1,0:T(8,128)(2,1)} %get-tuple-element.110), channel_id=1, source_target_pairs={{2,0},{4,2},{6,4},{3,1},{5,3},{7,5},{10,8},{12,10},{14,12},{11,9},... | collective-permute-start | bytes 147464 | tf_op jit(solution)/shard_map/ppermute | solution.py:25
  309.3 11.8 %copy-start.10 = (f32[3,32,64,128]{3,2,1,0:T(8,128)S(1)}, f32[3,32,64,128]{3,2,1,0:T(8,128)}, u32[]{:S(2)}) copy-start(f32[3,32,64,128]{3,2,1,0:T(8,128)} %get-tuple-element.178) | copy-start | bytes 9437188
  309.3 11.8 %slice-start.9 = ((s8[14155776]{0:T(1024)(128)(4,1)}), s8[4194304]{0:T(1024)(128)(4,1)S(1)}, s32[]{:S(2)}) async-start(s8[14155776]{0:T(1024)(128)(4,1)} %bitcast.178), calls=%async_computation.22 | async-start | bytes 8388608
  309.3 11.8 %slice-start.10 = ((s8[14155776]{0:T(1024)(128)(4,1)}), s8[4194304]{0:T(1024)(128)(4,1)S(1)}, s32[]{:S(2)}) async-start(s8[14155776]{0:T(1024)(128)(4,1)} %bitcast.178), calls=%async_computation.23 | async-start | bytes 8388608
  309.3 11.8 %slice-start.11 = ((s8[14155776]{0:T(1024)(128)(4,1)}), s8[1572864]{0:T(1024)(128)(4,1)S(1)}, s32[]{:S(2)}) async-start(s8[14155776]{0:T(1024)(128)(4,1)} %bitcast.178), calls=%async_computation.24 | async-start | bytes 3145728
  328.6 75.5 %all-reduce.23.cloned.1.call-start = ((), (), s32[]{:S(2)}) async-start(), calls=%async_computation.6 | async-start | bytes 1572864 | tf_op jit(solution)/shard_map/psum | solution.py:10
  331.4 47.8 %copy-start.4 = (bf16[3,32,64,128]{3,2,1,0:T(8,128)(2,1)}, bf16[3,32,64,128]{3,2,1,0:T(8,128)(2,1)S(1)}, u32[]{:S(2)}) copy-start(bf16[3,32,64,128]{3,2,1,0:T(8,128)(2,1)S(1)} %multiply_convert_fusion) | copy-start | bytes 4718596
  332.1 34.8 %collective-permute-start.28 = (bf16[3,1,64,128]{3,2,1,0:T(8,128)(2,1)}, bf16[3,1,64,128]{3,2,1,0:T(8,128)(2,1)S(1)}, u32[]{:S(2)}, u32[]{:S(2)}) collective-permute-start(bf16[3,1,64,128]{3,2,1,0:T(8,128)(2,1)} %get-tuple-element.107), channel_id=1, source_target_pairs={{0,2},{2,4},{4,6},{1,3},{3,5},{5,7},{8,10},{10,12},{12,14},{9,11},... | collective-permute-start | bytes 147464 | tf_op jit(solution)/shard_map/ppermute | solution.py:24
  335.2 31.7 %collective-permute-start.29 = (bf16[3,1,64,128]{3,2,1,0:T(8,128)(2,1)}, bf16[3,1,64,128]{3,2,1,0:T(8,128)(2,1)S(1)}, u32[]{:S(2)}, u32[]{:S(2)}) collective-permute-start(bf16[3,1,64,128]{3,2,1,0:T(8,128)(2,1)} %get-tuple-element.108), channel_id=1, source_target_pairs={{2,0},{4,2},{6,4},{3,1},{5,3},{7,5},{10,8},{12,10},{14,12},{11,9},... | collective-permute-start | bytes 147464 | tf_op jit(solution)/shard_map/ppermute | solution.py:25
  338.0 36.8 %collective-permute-start.27 = (bf16[3,34,1,128]{3,2,1,0:T(2,128)(2,1)}, bf16[3,34,1,128]{3,2,1,0:T(2,128)(2,1)S(1)}, u32[]{:S(2)}, u32[]{:S(2)}) collective-permute-start(bf16[3,34,1,128]{3,2,1,0:T(2,128)(2,1)} %get-tuple-element.81), channel_id=1, source_target_pairs={{1,0},{3,2},{5,4},{7,6},{9,8},{11,10},{13,12},{15,14},{17,16},{19,... | collective-permute-start | bytes 78344 | tf_op jit(solution)/shard_map/ppermute | solution.py:25
  339.3 35.5 %collective-permute-start.26 = (bf16[3,34,1,128]{3,2,1,0:T(2,128)(2,1)}, bf16[3,34,1,128]{3,2,1,0:T(2,128)(2,1)}, u32[]{:S(2)}, u32[]{:S(2)}) collective-permute-start(bf16[3,34,1,128]{3,2,1,0:T(2,128)(2,1)} %get-tuple-element.82), channel_id=1, source_target_pairs={{0,1},{2,3},{4,5},{6,7},{8,9},{10,11},{12,13},{14,15},{16,17},{18,... | collective-permute-start | bytes 78344 | tf_op jit(solution)/shard_map/ppermute | solution.py:24
  366.7 152.1 %all-reduce.29.cloned.1.call-start = ((), (), s32[]{:S(2)}) async-start(), calls=%async_computation.9 | async-start | bytes 1572864 | tf_op jit(solution)/shard_map/psum | solution.py:10
  366.9 12.2 %copy-start.46 = (bf16[3,1,64,128]{3,2,1,0:T(8,128)(2,1)}, bf16[3,1,64,128]{3,2,1,0:T(8,128)(2,1)S(1)}, u32[]{:S(2)}) copy-start(bf16[3,1,64,128]{3,2,1,0:T(8,128)(2,1)S(1)} %collective-permute-done.28) | copy-start | bytes 147460
  366.9 12.2 %copy-start.44 = (bf16[3,1,64,128]{3,2,1,0:T(8,128)(2,1)}, bf16[3,1,64,128]{3,2,1,0:T(8,128)(2,1)S(1)}, u32[]{:S(2)}) copy-start(bf16[3,1,64,128]{3,2,1,0:T(8,128)(2,1)S(1)} %collective-permute-done.29) | copy-start | bytes 147460
  367.7 229.5 %collective-permute-start.31 = (bf16[3,34,1,128]{3,2,1,0:T(2,128)(2,1)}, bf16[3,34,1,128]{3,2,1,0:T(2,128)(2,1)}, u32[]{:S(2)}, u32[]{:S(2)}) collective-permute-start(bf16[3,34,1,128]{3,2,1,0:T(2,128)(2,1)} %get-tuple-element.77), channel_id=1, source_target_pairs={{1,0},{3,2},{5,4},{7,6},{9,8},{11,10},{13,12},{15,14},{17,16},{19,... | collective-permute-start | bytes 78344 | tf_op jit(solution)/shard_map/ppermute | solution.py:25
  369.0 228.3 %collective-permute-start.30 = (bf16[3,34,1,128]{3,2,1,0:T(2,128)(2,1)}, bf16[3,34,1,128]{3,2,1,0:T(2,128)(2,1)}, u32[]{:S(2)}, u32[]{:S(2)}) collective-permute-start(bf16[3,34,1,128]{3,2,1,0:T(2,128)(2,1)} %get-tuple-element.78), channel_id=1, source_target_pairs={{0,1},{2,3},{4,5},{6,7},{8,9},{10,11},{12,13},{14,15},{16,17},{18,... | collective-permute-start | bytes 78344 | tf_op jit(solution)/shard_map/ppermute | solution.py:24
  413.1 6.4 collective-permute-start.20
  414.4 6.4 collective-permute-start.21
  415.8 8.6 %collective-permute-start.8 = (bf16[3,1,64,128]{3,2,1,0:T(8,128)(2,1)S(1)}, bf16[3,1,64,128]{3,2,1,0:T(8,128)(2,1)S(1)}, u32[]{:S(2)}, u32[]{:S(2)}) collective-permute-start(bf16[3,1,64,128]{3,2,1,0:T(8,128)(2,1)S(1)} %get-tuple-element.113), channel_id=1, source_target_pairs={{0,2},{2,4},{4,6},{1,3},{3,5},{5,7},{8,10},{10,12},{12,14},{9,11},... | collective-permute-start | bytes 147464 | tf_op jit(solution)/shard_map/ppermute | solution.py:24
  419.5 6.2 collective-permute-start.9
  420.9 9.4 %collective-permute-start.23 = (bf16[3,34,1,128]{3,2,1,0:T(2,128)(2,1)S(1)}, bf16[3,34,1,128]{3,2,1,0:T(2,128)(2,1)S(1)}, u32[]{:S(2)}, u32[]{:S(2)}) collective-permute-start(bf16[3,34,1,128]{3,2,1,0:T(2,128)(2,1)S(1)} %get-tuple-element.89), channel_id=1, source_target_pairs={{0,1},{2,3},{4,5},{6,7},{8,9},{10,11},{12,13},{14,15},{16,17},{18,... | collective-permute-start | bytes 78344 | tf_op jit(solution)/shard_map/ppermute | solution.py:24
  424.4 7.3 collective-permute-start.22
  425.8 13.4 %collective-permute-start.11 = (bf16[3,34,1,128]{3,2,1,0:T(2,128)(2,1)S(1)}, bf16[3,34,1,128]{3,2,1,0:T(2,128)(2,1)S(1)}, u32[]{:S(2)}, u32[]{:S(2)}) collective-permute-start(bf16[3,34,1,128]{3,2,1,0:T(2,128)(2,1)S(1)} %get-tuple-element.85), channel_id=1, source_target_pairs={{0,1},{2,3},{4,5},{6,7},{8,9},{10,11},{12,13},{14,15},{16,17},{18,... | collective-permute-start | bytes 78344 | tf_op jit(solution)/shard_map/ppermute | solution.py:24
  430.4 8.9 %collective-permute-start.10 = (bf16[3,34,1,128]{3,2,1,0:T(2,128)(2,1)S(1)}, bf16[3,34,1,128]{3,2,1,0:T(2,128)(2,1)S(1)}, u32[]{:S(2)}, u32[]{:S(2)}) collective-permute-start(bf16[3,34,1,128]{3,2,1,0:T(2,128)(2,1)S(1)} %get-tuple-element.86), channel_id=1, source_target_pairs={{1,0},{3,2},{5,4},{7,6},{9,8},{11,10},{13,12},{15,14},{17,16},{19,... | collective-permute-start | bytes 78344 | tf_op jit(solution)/shard_map/ppermute | solution.py:25
  479.7 76.7 %all-reduce.21.cloned.1.call-start = ((), (), s32[]{:S(2)}) async-start(), calls=%async_computation.5 | async-start | bytes 1572864 | tf_op jit(solution)/shard_map/psum | solution.py:10
  518.8 146.7 %reduce-scatter.3.cloned.1.call-start = ((), (), s32[]{:S(2)}) async-start(), calls=%async_computation.2 | async-start | bytes 5242880 | tf_op jit(solution)/shard_map/reduce_scatter | solution.py:185
  588.6 215.4 %all-reduce.19.cloned.1.call-start = ((), (), s32[]{:S(2)}) async-start(), calls=%async_computation.4 | async-start | bytes 2359296 | tf_op jit(solution)/shard_map/psum | solution.py:194
  606.7 8.0 copy-start.29
  614.7 15.0 %slice-start = ((s8[14155776]{0:T(1024)(128)(4,1)}), s8[4194304]{0:T(1024)(128)(4,1)S(1)}, s32[]{:S(2)}) async-start(s8[14155776]{0:T(1024)(128)(4,1)} %bitcast.154), calls=%async_computation.13 | async-start | bytes 8388608
  614.7 15.0 %slice-start.1 = ((s8[14155776]{0:T(1024)(128)(4,1)}), s8[4194304]{0:T(1024)(128)(4,1)S(1)}, s32[]{:S(2)}) async-start(s8[14155776]{0:T(1024)(128)(4,1)} %bitcast.154), calls=%async_computation.14 | async-start | bytes 8388608
  622.1 11.6 %slice-start.4 = ((s8[14155776]{0:T(1024)(128)(4,1)}), s8[4194304]{0:T(1024)(128)(4,1)S(1)}, s32[]{:S(2)}) async-start(s8[14155776]{0:T(1024)(128)(4,1)} %bitcast.156), calls=%async_computation.17 | async-start | bytes 8388608
  622.1 11.6 %slice-start.5 = ((s8[14155776]{0:T(1024)(128)(4,1)}), s8[4194304]{0:T(1024)(128)(4,1)S(1)}, s32[]{:S(2)}) async-start(s8[14155776]{0:T(1024)(128)(4,1)} %bitcast.156), calls=%async_computation.18 | async-start | bytes 8388608
  638.8 70.6 %copy-start.31 = (bf16[384,2048]{1,0:T(8,128)(2,1)S(1)}, bf16[384,2048]{1,0:T(8,128)(2,1)}, u32[]{:S(2)}) copy-start(bf16[384,2048]{1,0:T(8,128)(2,1)} %reshape.166) | copy-start | bytes 4718596
  638.8 209.1 %reduce-scatter.5.cloned.1.call-start = ((), (), s32[]{:S(2)}) async-start(), calls=%async_computation.3 | async-start | bytes 2359296 | tf_op jit(solution)/shard_map/reduce_scatter | solution.py:193
  (53 other events, 221.3 us)
Sparse Core Ops, SparseCore 0:
  55.2 38.6 all-reduce.34
  109.9 39.2 all-reduce.26
  223.9 36.9 all-reduce.32
  263.4 34.9 all-reduce.24
  328.7 37.9 all-reduce.30
  369.1 34.9 all-reduce.22
  479.8 38.9 all-reduce.28
  521.4 34.9 all-reduce.20
  588.7 76.7 reduce-scatter.2
  671.3 132.6 all-reduce.18
  807.9 40.0 reduce-scatter.4
